TPU v7x, 256 devices: a whole 4x4x8 slice. The times are simulated.
256 devices in a mesh: prow: 8 (over z_lo, y), pcol: 32 (over z_hi, x, core).
Axes of the slice: x: 4, y: 4, z: 8 (z_hi: 4, z_lo: 2; z = z_hi * 2 + z_lo), core: 2. Of those that a mesh axis runs over, the one named last changes fastest.
Arguments:
- ancestor_inverse: bfloat16 [24576, 24576], P('prow', 'pcol'), may hold values from -6 to 6
- tile_pattern: int32 [64, 64], replicated, may hold values 0 or 1
- rows_first: int32 [24576], replicated, may hold values 0 or 1
- rows_second: int32 [24576], replicated, may hold values 0 or 1
- panel_first: bfloat16 [24576, 512], P('prow', 'pcol'), may hold values from -0.0390625 to 0.0390625
- panel_second: bfloat16 [24576, 512], P('prow', 'pcol'), may hold values from -0.21875 to 0.21875
- inner_panel: bfloat16 [512, 512], replicated, may hold values from -0.25 to 0.25
- pivot_first: float32 [512, 512], replicated, may hold values from -6 to 6
- pivot_second: float32 [512, 512], replicated, may hold values from -6 to 6
Outputs:
- column_first: bfloat16 [24576, 512], P(('prow', 'pcol'))
- diagonal_first: float32 [512, 512], replicated
- inner_second: float32 [512, 512], replicated
- column_second: bfloat16 [24576, 512], P(('prow', 'pcol'))
- diagonal_second: float32 [512, 512], replicated
Inputs may be any that keep to these rules, and one draw needn't show every extreme that they name: `tile_pattern`: 1 marks a structurally nonzero tile. `rows_first`: 1 marks a row of the first supernode's structure. By construction here, a row belongs to the second supernode's structure only where both rows_second and rows_first are 1.
All inputs are finite; a program needn't handle non-finite values.
Results may differ from a plain program's by a relative error of at most 0.015.
Values may be sent and summed in bfloat16 or wider, within the bound.
A program may use at most 128 MiB of HBM per device.

v0:
```python
import jax
import jax.numpy as jnp
from jax import lax
from jax.sharding import PartitionSpec as P

TILE = 384


def from_root(shard, axis, root):
    mine = lax.axis_index(axis) == root
    return lax.psum(jnp.where(mine, shard, jnp.zeros_like(shard)), axis)


def mask_tiles(block, pattern, row_start, col_start):
    tile_rows = block.shape[0] // TILE
    tile_cols = block.shape[1] // TILE
    window = lax.dynamic_slice(pattern, (row_start, col_start), (tile_rows, tile_cols)).astype(
        jnp.bfloat16
    )
    shaped = block.reshape(tile_rows, TILE, tile_cols, TILE) * window[:, None, :, None]
    return shaped.reshape(block.shape)


def body(
    ancestor_inverse,
    tile_pattern,
    rows_first,
    rows_second,
    panel_first,
    panel_second,
    inner_panel,
    pivot_first,
    pivot_second,
):
    row_count = lax.axis_size("prow")
    col_count = lax.axis_size("pcol")
    row_id = lax.axis_index("prow")
    col_id = lax.axis_index("pcol")
    row_block = ancestor_inverse.shape[0]
    col_block = ancestor_inverse.shape[1]
    share = row_block // col_count
    sparse = mask_tiles(
        ancestor_inverse, tile_pattern, row_id * (row_block // TILE), col_id * (col_block // TILE)
    )
    struct_first = lax.dynamic_slice_in_dim(rows_first, row_id * row_block, row_block).astype(
        jnp.bfloat16
    )
    struct_second = struct_first * lax.dynamic_slice_in_dim(
        rows_second, row_id * row_block, row_block
    ).astype(jnp.bfloat16)
    local_first = panel_first * struct_first[:, None]
    local_second = panel_second * struct_second[:, None]
    source = col_id * row_count // col_count
    offset = col_id * col_block - source * row_block

    def summed_terms(columns):
        return jnp.dot(sparse, columns, preferred_element_type=jnp.float32)

    def ancestor_terms(local):
        full = lax.all_gather(local, "pcol", axis=1, tiled=True)
        mirrored = from_root(lax.dynamic_slice_in_dim(full, offset, col_block, 0), "prow", source)
        return (
            full,
            lax.psum_scatter(
                summed_terms(mirrored).astype(jnp.bfloat16), "pcol", scatter_dimension=0, tiled=True
            ).astype(jnp.float32),
        )

    full_first, sum_first = ancestor_terms(local_first)
    full_second, sum_second = ancestor_terms(local_second)
    column_first = (-sum_first).astype(jnp.bfloat16)
    own_first = lax.dynamic_slice_in_dim(full_first, col_id * share, share, 0)
    own_second = lax.dynamic_slice_in_dim(full_second, col_id * share, share, 0)
    corr_first, crossed = lax.psum(
        (
            jnp.dot(own_first.T, column_first, preferred_element_type=jnp.float32),
            jnp.dot(column_first.T, own_second, preferred_element_type=jnp.float32),
        ),
        ("prow", "pcol"),
    )
    diagonal_first = pivot_first - corr_first
    column_second = (
        -(sum_second + jnp.dot(column_first, inner_panel, preferred_element_type=jnp.float32))
    ).astype(jnp.bfloat16)
    inner_wide = inner_panel.astype(jnp.float32)
    inner_second = -(jnp.dot(diagonal_first, inner_wide, precision=lax.Precision.HIGHEST) + crossed)
    corr_second = lax.psum(
        jnp.dot(own_second.T, column_second, preferred_element_type=jnp.float32), ("prow", "pcol")
    )
    diagonal_second = (
        pivot_second
        - jnp.dot(inner_wide.T, inner_second, precision=lax.Precision.HIGHEST)
        - corr_second
    )
    return (column_first, diagonal_first, inner_second, column_second, diagonal_second)


def solution(mesh):
    return jax.shard_map(
        body,
        mesh=mesh,
        in_specs=(
            P("prow", "pcol"),
            P(),
            P(),
            P(),
            P("prow", "pcol"),
            P("prow", "pcol"),
            P(),
            P(),
            P(),
        ),
        out_specs=(P(("prow", "pcol"), None), P(), P(), P(("prow", "pcol"), None), P()),
        check_vma=False,
    )
```

profile of v0, /device:TPU:8, one launch (start us, length us, event | category | flops | bytes accessed | tf_op | source)
XLA Modules:
  0.0 701.2 jit_solution(2915164507721282915)
XLA Ops:
  7.2 0.0 copy-start
  7.2 0.0 all-gather.5.cloned.1.call-start
  7.2 0.8 fusion.13
  8.0 1.5 broadcast_multiply_fusion
  9.6 0.0 all-gather.5.cloned.1.call-update
  9.6 0.0 all-gather.3.cloned.1.call-start
  9.6 1.5 broadcast_multiply_fusion.1
  11.2 0.0 all-gather.3.cloned.1.call-update
  11.2 0.0 all-reduce.7.cloned.1.call-start
  11.3 59.7 %all-gather.5.cloned.1.call-done = bf16[3072,512]{0,1:T(8,128)(2,1)} async-done(((bf16[3072,16]{0,1:T(8,128)(2,1)}), bf16[3072,512]{0,1:T(8,128)(2,1)}) %all-gather.5.cloned.1.call-update) | async-done | bytes 3145744 | tf_op jit(solution)/shard_map/all_gather | solution.py:60
  71.0 2.1 dynamic-slice_select_fusion
  73.2 55.8 %all-gather.3.cloned.1.call-done = bf16[3072,512]{0,1:T(8,128)(2,1)} async-done(((bf16[3072,16]{0,1:T(8,128)(2,1)}), bf16[3072,512]{0,1:T(8,128)(2,1)}) %all-gather.3.cloned.1.call-update) | async-done | bytes 3145744 | tf_op jit(solution)/shard_map/all_gather | solution.py:60
  129.0 2.1 dynamic-slice_select_fusion.1
  131.1 0.0 all-reduce.7.cloned.1.call-update
  131.2 0.0 reduce-scatter.3.cloned.1.call-start
  131.2 0.8 dynamic-slice_convert_fusion.2
  132.0 2.5 mul.55
  134.5 3.0 copy.18
  137.5 76.0 %all-reduce.7.cloned.1.call-done = (bf16[768,512]{0,1:T(8,128)(2,1)}, bf16[768,512]{0,1:T(8,128)(2,1)}) async-done(((bf16[768,512]{0,1:T(8,128)(2,1)}, bf16[768,512]{0,1:T(8,128)(2,1)}), (bf16[768,512]{0,1:T(8,128)(2,1)}, bf16[768,512]{0,1:T(8,128)(2,1)})) %all-reduce.7.cloned.1.call-update) | async-done | bytes 1572880 | tf_op jit(solution)/shard_map/psum | solution.py:11
  213.4 8.4 %convolution_convert_fusion.1 = bf16[3072,512]{1,0:T(8,128)(2,1)} fusion(bf16[768,512]{0,1:T(8,128)(2,1)} %get-tuple-element.13, bf16[3072,768]{1,0:T(8,128)(2,1)} %param.9, bf16[3072,768]{1,0:T(8,128)(2,1)} %bitcast.21), kind=kOutput, calls=%fused_computation.1 | convolution fusion | flops 2419851264 | bytes 13369344 | tf_op jit(solution)/shard_map/dot_general | solution.py:57
  221.8 0.0 reduce-scatter.3.cloned.1.call-update
  221.8 0.0 reduce-scatter.5.cloned.1.call-start
  221.9 7.9 %convolution_convert_fusion = bf16[3072,512]{1,0:T(8,128)(2,1)} fusion(bf16[768,512]{0,1:T(8,128)(2,1)S(1)} %copy-done.9, bf16[3072,768]{1,0:T(8,128)(2,1)} %param.9, bf16[3072,768]{1,0:T(8,128)(2,1)} %bitcast.22), kind=kOutput, calls=%fused_computation | convolution fusion | flops 2419851264 | bytes 13369344 | tf_op jit(solution)/shard_map/dot_general | solution.py:57
  229.8 0.0 reduce-scatter.5.cloned.1.call-update
  229.8 0.0 copy-start.6
  229.8 0.2 all-reduce.5.cloned.1.call-start
  230.0 88.8 %reduce-scatter.3.cloned.1.call-done = bf16[96,512]{1,0:T(8,128)(2,1)} async-done(((bf16[3072,512]{1,0:T(8,128)(2,1)}), bf16[96,512]{1,0:T(8,128)(2,1)}) %reduce-scatter.3.cloned.1.call-update) | async-done | bytes 98320 | tf_op jit(solution)/shard_map/reduce_scatter | solution.py:64
  318.8 0.9 negate_convert_fusion
  319.8 0.0 copy-start.4
  319.8 0.0 copy-start.5
  319.8 2.4 fusion.11
  322.2 2.3 fusion.7
  324.4 91.8 %reduce-scatter.5.cloned.1.call-done = bf16[96,512]{1,0:T(8,128)(2,1)} async-done(((bf16[3072,512]{1,0:T(8,128)(2,1)}), bf16[96,512]{1,0:T(8,128)(2,1)}) %reduce-scatter.5.cloned.1.call-update) | async-done | bytes 98320 | tf_op jit(solution)/shard_map/reduce_scatter | solution.py:64
  416.3 0.0 copy-done
  416.3 1.1 fusion.6
  417.4 0.0 copy-start.8
  417.4 2.4 fusion.9
  419.8 0.0 all-reduce.5.cloned.1.call-update
  419.8 0.0 copy-done.6
  419.8 1.3 copy.14
  421.1 264.4 %all-reduce.5.cloned.1.call-done = (f32[512,512]{1,0:T(8,128)}, f32[512,512]{1,0:T(8,128)}, f32[512,512]{0,1:T(8,128)}) async-done(((f32[512,512]{1,0:T(8,128)}, f32[512,512]{1,0:T(8,128)}, f32[512,512]{0,1:T(8,128)}), (f32[512,512]{1,0:T(8,128)}, f32[512,512]{1,0:T(8,128)}, f32[512,512]{0,1:T(8,128)})) %all-reduce.5.cloned.1.call-update) | async-done | bytes 3145744 | tf_op jit(solution)/shard_map/psum | solution.py:74
  685.6 1.6 sub.18
  687.2 0.0 copy-done.8
  687.2 0.0 copy-start.1
  687.2 2.6 fusion.2
  689.8 0.0 copy-start.2
  689.8 2.0 fusion.4
  691.8 2.5 copy.16
  (10 shorter events, 0.0 us)
Async XLA Ops:
  7.2 409.1 %copy-start = (bf16[512,512]{1,0:T(8,128)(2,1)S(1)}, bf16[512,512]{1,0:T(8,128)(2,1)}, u32[]{:S(2)}) copy-start(bf16[512,512]{1,0:T(8,128)(2,1)} %param.15) | copy-start | bytes 1572868
  7.2 63.8 %all-gather.5.cloned.1.call-start = ((), (), s32[]{:S(2)}) async-start(), calls=%async_computation.4 | async-start | bytes 3244032 | tf_op jit(solution)/shard_map/all_gather | solution.py:60
  9.6 119.4 %all-gather.3.cloned.1.call-start = ((), (), s32[]{:S(2)}) async-start(), calls=%async_computation.2 | async-start | bytes 3244032 | tf_op jit(solution)/shard_map/all_gather | solution.py:60
  11.2 202.2 %all-reduce.7.cloned.1.call-start = ((), (), s32[]{:S(2)}) async-start(), calls=%async_computation.7 | async-start | bytes 3145728 | tf_op jit(solution)/shard_map/psum | solution.py:11
  131.2 187.7 %reduce-scatter.3.cloned.1.call-start = ((), (), s32[]{:S(2)}) async-start(), calls=%async_computation.3 | async-start | bytes 3244032 | tf_op jit(solution)/shard_map/reduce_scatter | solution.py:64
  213.4 8.4 %copy-start.9 = (bf16[768,512]{0,1:T(8,128)(2,1)S(1)}, bf16[768,512]{0,1:T(8,128)(2,1)}, u32[]{:S(2)}) copy-start(bf16[768,512]{0,1:T(8,128)(2,1)} %get-tuple-element.14) | copy-start | bytes 2359300
  221.8 194.4 %reduce-scatter.5.cloned.1.call-start = ((), (), s32[]{:S(2)}) async-start(), calls=%async_computation.5 | async-start | bytes 3244032 | tf_op jit(solution)/shard_map/reduce_scatter | solution.py:64
  229.8 190.0 %copy-start.6 = (f32[512,512]{1,0:T(8,128)S(1)}, f32[512,512]{1,0:T(8,128)}, u32[]{:S(2)}) copy-start(f32[512,512]{1,0:T(8,128)} %param.17) | copy-start | bytes 3145732
  229.8 455.8 %all-reduce.5.cloned.1.call-start = ((), (), s32[]{:S(2)}) async-start(), calls=%async_computation.6 | async-start | bytes 6291456 | tf_op jit(solution)/shard_map/psum | solution.py:74
  319.8 101.4 %copy-start.4 = (bf16[96,512]{1,0:T(8,128)(2,1)}, bf16[96,512]{1,0:T(8,128)(2,1)S(1)}, u32[]{:S(2)}) copy-start(bf16[96,512]{1,0:T(8,128)(2,1)S(1)} %negate_convert_fusion) | copy-start | bytes 294916
  319.8 365.8 %copy-start.5 = (f32[512,512]{1,0:T(8,128)S(1)}, f32[512,512]{1,0:T(8,128)}, u32[]{:S(2)}) copy-start(f32[512,512]{1,0:T(8,128)} %param.16) | copy-start | bytes 3145732
  417.4 269.8 %copy-start.8 = (bf16[96,512]{1,0:T(8,128)(2,1)}, bf16[96,512]{1,0:T(8,128)(2,1)S(1)}, u32[]{:S(2)}) copy-start(bf16[96,512]{1,0:T(8,128)(2,1)S(1)} %fusion.6) | copy-start | bytes 294916
  685.6 4.2 copy-start.3
  685.6 4.2 copy-start.7
  687.2 7.2 %copy-start.1 = (f32[512,512]{1,0:T(8,128)}, f32[512,512]{1,0:T(8,128)S(1)}, u32[]{:S(2)}) copy-start(f32[512,512]{1,0:T(8,128)S(1)} %sub.18) | copy-start | bytes 3145732
  689.8 4.6 copy-start.2
Sparse Core Ops, SparseCore 0:
  11.1 59.8 all-gather.4
  74.1 54.8 all-gather.2
  132.3 81.1 all-reduce.6
  222.0 96.8 reduce-scatter.2
  323.1 93.1 reduce-scatter.4
  422.5 263.0 all-reduce.4
where the time goes:
time: 702 us; the launch traced here: 701 us
  waiting for transfers between devices  637 us (91%)
  matrix products  29 us (4%)
  between operations  14.3 us (2%)
  other arithmetic  11.4 us (2%)
  local copies, waits for them, and re-layouts  9.39 us (1%)
    psum x1, waiting for transfers between devices, body(): lax.psum((jnp.dot(own_first.T, column_first, preferred_element_type=jnp.f...  264 us
    reduce_scatter x2, waiting for transfers between devices, ancestor_terms(): lax.psum_scatter(summed_terms(mirrored).astype(jnp.bfloat16), 'pcol', sca...  181 us
    all_gather x2, waiting for transfers between devices, ancestor_terms(): full = lax.all_gather(local, 'pcol', axis=1, tiled=True)  116 us
    psum x1, waiting for transfers between devices, from_root(): return lax.psum(jnp.where(mine, shard, jnp.zeros_like(shard)), axis)  76 us
    dot_general x2, matrix products, summed_terms(): return jnp.dot(sparse, columns, preferred_element_type=jnp.float32)  16.2 us
  transfers between devices with their start and end apart: 6, of which 6 were waited for; matrix products, arithmetic and copies ran while one was open for 4% of the time, Pallas kernels for 0%

commit v1 on v0

--- a/solution.py
+++ b/solution.py
@@ -57,7 +57,9 @@
         return jnp.dot(sparse, columns, preferred_element_type=jnp.float32)
 
     def ancestor_terms(local):
-        full = lax.all_gather(local, "pcol", axis=1, tiled=True)
+        full = jnp.concatenate(
+            lax.all_to_all(jnp.stack([local] * lax.axis_size("pcol")), "pcol", 0, 0), axis=1
+        )
         mirrored = from_root(lax.dynamic_slice_in_dim(full, offset, col_block, 0), "prow", source)
         return (
             full,

time: 702 us -> 749 us (1.067)
  waiting for transfers between devices: 637 us -> 661 us
  starting transfers between devices: 0.43 us -> 20.8 us
    all_to_all x0 -> x2, waiting for transfers between devices: none -> 134 us  [ancestor_terms(): lax.all_to_all(jnp.stack([local] * lax.axis_size('pcol')), 'pcol', 0, 0)]
    all_gather x2 -> x0, waiting for transfers between devices: 116 us -> none  [ancestor_terms(): full = lax.all_gather(local, 'pcol', axis=1, tiled=True)]
    all_to_all x0 -> x2, starting transfers between devices: none -> 20.4 us  [ancestor_terms(): lax.all_to_all(jnp.stack([local] * lax.axis_size('pcol')), 'pcol', 0, 0)]
  transfers between devices with their start and end apart: 6 -> 6, of which waited for: 6 -> 6; matrix products, arithmetic and copies ran while one was open for 4% -> 3% of each run, Pallas kernels for 0% -> 0%
where the time goes in v1:
time: 749 us; the launch traced here: 748 us
  waiting for transfers between devices  661 us (88%)
  matrix products  29 us (4%)
  starting transfers between devices  20.8 us (3%)
  between operations  14 us (2%)
  local copies, waits for them, and re-layouts  13.5 us (2%)
  other arithmetic  9.26 us (1%)
    psum x1, waiting for transfers between devices, body(): lax.psum((jnp.dot(own_first.T, column_first, preferred_element_type=jnp.f...  265 us
    reduce_scatter x2, waiting for transfers between devices, ancestor_terms(): lax.psum_scatter(summed_terms(mirrored).astype(jnp.bfloat16), 'pcol', sca...  181 us
    all_to_all x2, waiting for transfers between devices, ancestor_terms(): lax.all_to_all(jnp.stack([local] * lax.axis_size('pcol')), 'pcol', 0, 0)  134 us
    psum x1, waiting for transfers between devices, from_root(): return lax.psum(jnp.where(mine, shard, jnp.zeros_like(shard)), axis)  82 us
    all_to_all x2, starting transfers between devices, ancestor_terms(): lax.all_to_all(jnp.stack([local] * lax.axis_size('pcol')), 'pcol', 0, 0)  20.4 us
    dot_general x2, matrix products, summed_terms(): return jnp.dot(sparse, columns, preferred_element_type=jnp.float32)  16.2 us
  transfers between devices with their start and end apart: 6, of which 6 were waited for; matrix products, arithmetic and copies ran while one was open for 3% of the time, Pallas kernels for 0%

profile of v1, /device:TPU:8, one launch (start us, length us, event | category | flops | bytes accessed | tf_op | source)
XLA Modules:
  0.0 747.9 jit_solution(10614096061967909996)
XLA Ops:
  7.2 0.0 copy-start
  7.2 0.8 fusion.13
  8.0 0.9 broadcast_multiply_fusion
  8.9 0.0 copy-start.9
  8.9 2.0 stack.5
  10.9 11.4 %all-to-all-start.1 = ((bf16[32,3072,16]{1,2,0:T(8,128)(2,1)}), bf16[32,3072,16]{1,2,0:T(8,128)(2,1)}, u32[]{:S(2)}, u32[]{:S(2)}) async-start(bf16[32,3072,16]{1,2,0:T(8,128)(2,1)} %stack.5), calls=%async_computation.2 | async-start | bytes 6291456 | tf_op jit(solution)/shard_map/all_to_all | solution.py:61
  22.4 69.7 %all-to-all-done.1 = bf16[32,3072,16]{1,2,0:T(8,128)(2,1)} async-done(((bf16[32,3072,16]{1,2,0:T(8,128)(2,1)}), bf16[32,3072,16]{1,2,0:T(8,128)(2,1)}, u32[]{:S(2)}, u32[]{:S(2)}) %all-to-all-start.1) | async-done | bytes 3145760 | tf_op jit(solution)/shard_map/all_to_all | solution.py:61
  92.1 2.0 stack.4
  94.1 9.0 %all-to-all-start = ((bf16[32,3072,16]{1,2,0:T(8,128)(2,1)}), bf16[32,3072,16]{1,2,0:T(8,128)(2,1)}, u32[]{:S(2)}, u32[]{:S(2)}) async-start(bf16[32,3072,16]{1,2,0:T(8,128)(2,1)} %stack.4), calls=%async_computation | async-start | bytes 6291456 | tf_op jit(solution)/shard_map/all_to_all | solution.py:61
  103.1 0.0 all-reduce.7.cloned.1.call-start
  103.2 2.1 dynamic-slice_select_fusion
  105.3 64.2 %all-to-all-done = bf16[32,3072,16]{1,2,0:T(8,128)(2,1)} async-done(((bf16[32,3072,16]{1,2,0:T(8,128)(2,1)}), bf16[32,3072,16]{1,2,0:T(8,128)(2,1)}, u32[]{:S(2)}, u32[]{:S(2)}) %all-to-all-start) | async-done | bytes 3145760 | tf_op jit(solution)/shard_map/all_to_all | solution.py:61
  169.6 2.1 dynamic-slice_select_fusion.1
  171.7 0.0 all-reduce.7.cloned.1.call-update
  171.7 0.0 reduce-scatter.3.cloned.1.call-start
  171.8 0.8 dynamic-slice_convert_fusion.2
  172.6 2.5 mul.55
  175.1 3.0 copy.23
  178.0 82.0 %all-reduce.7.cloned.1.call-done = (bf16[768,512]{0,1:T(8,128)(2,1)}, bf16[768,512]{0,1:T(8,128)(2,1)}) async-done(((bf16[768,512]{0,1:T(8,128)(2,1)}, bf16[768,512]{0,1:T(8,128)(2,1)}), (bf16[768,512]{0,1:T(8,128)(2,1)}, bf16[768,512]{0,1:T(8,128)(2,1)})) %all-reduce.7.cloned.1.call-update) | async-done | bytes 1572880 | tf_op jit(solution)/shard_map/psum | solution.py:11
  260.1 8.4 %convolution_convert_fusion.1 = bf16[3072,512]{1,0:T(8,128)(2,1)} fusion(bf16[768,512]{0,1:T(8,128)(2,1)} %get-tuple-element.18, bf16[3072,768]{1,0:T(8,128)(2,1)} %param.9, bf16[3072,768]{1,0:T(8,128)(2,1)} %bitcast.27), kind=kOutput, calls=%fused_computation.1 | convolution fusion | flops 2419851264 | bytes 13369344 | tf_op jit(solution)/shard_map/dot_general | solution.py:57
  268.5 0.0 reduce-scatter.3.cloned.1.call-update
  268.5 0.0 reduce-scatter.5.cloned.1.call-start
  268.5 7.9 %convolution_convert_fusion = bf16[3072,512]{1,0:T(8,128)(2,1)} fusion(bf16[768,512]{0,1:T(8,128)(2,1)S(1)} %copy-done.10, bf16[3072,768]{1,0:T(8,128)(2,1)} %param.9, bf16[3072,768]{1,0:T(8,128)(2,1)} %bitcast.28), kind=kOutput, calls=%fused_computation | convolution fusion | flops 2419851264 | bytes 13369344 | tf_op jit(solution)/shard_map/dot_general | solution.py:57
  276.4 0.0 reduce-scatter.5.cloned.1.call-update
  276.4 0.0 copy-start.6
  276.4 0.2 all-reduce.5.cloned.1.call-start
  276.7 88.9 %reduce-scatter.3.cloned.1.call-done = bf16[96,512]{1,0:T(8,128)(2,1)} async-done(((bf16[3072,512]{1,0:T(8,128)(2,1)}), bf16[96,512]{1,0:T(8,128)(2,1)}) %reduce-scatter.3.cloned.1.call-update) | async-done | bytes 98320 | tf_op jit(solution)/shard_map/reduce_scatter | solution.py:66
  365.6 0.9 negate_convert_fusion
  366.5 0.0 copy-start.4
  366.5 0.0 copy-start.5
  366.5 2.4 fusion.11
  368.9 2.3 fusion.7
  371.2 92.0 %reduce-scatter.5.cloned.1.call-done = bf16[96,512]{1,0:T(8,128)(2,1)} async-done(((bf16[3072,512]{1,0:T(8,128)(2,1)}), bf16[96,512]{1,0:T(8,128)(2,1)}) %reduce-scatter.5.cloned.1.call-update) | async-done | bytes 98320 | tf_op jit(solution)/shard_map/reduce_scatter | solution.py:66
  463.2 0.0 copy-done
  463.2 1.1 fusion.6
  464.3 0.0 copy-start.8
  464.4 2.4 fusion.9
  466.7 0.0 all-reduce.5.cloned.1.call-update
  466.7 1.3 copy.19
  468.1 264.5 %all-reduce.5.cloned.1.call-done = (f32[512,512]{1,0:T(8,128)}, f32[512,512]{1,0:T(8,128)}, f32[512,512]{0,1:T(8,128)}) async-done(((f32[512,512]{1,0:T(8,128)}, f32[512,512]{1,0:T(8,128)}, f32[512,512]{0,1:T(8,128)}), (f32[512,512]{1,0:T(8,128)}, f32[512,512]{1,0:T(8,128)}, f32[512,512]{0,1:T(8,128)})) %all-reduce.5.cloned.1.call-update) | async-done | bytes 3145744 | tf_op jit(solution)/shard_map/psum | solution.py:76
  732.6 1.6 sub.18
  734.2 0.0 copy-done.8
  734.2 0.0 copy-start.1
  734.2 2.6 fusion.2
  736.8 0.0 copy-start.2
  736.8 0.0 copy-done.3
  736.8 2.0 fusion.4
  738.9 2.5 copy.21
  (12 shorter events, 0.0 us)
Async XLA Ops:
  7.2 456.1 %copy-start = (bf16[512,512]{1,0:T(8,128)(2,1)S(1)}, bf16[512,512]{1,0:T(8,128)(2,1)}, u32[]{:S(2)}) copy-start(bf16[512,512]{1,0:T(8,128)(2,1)} %param.15) | copy-start | bytes 1572868
  8.9 13.5 %copy-start.9 = (bf16[3072,16]{0,1:T(8,128)(2,1)S(1)}, bf16[3072,16]{0,1:T(8,128)(2,1)}, u32[]{:S(2)}) copy-start(bf16[3072,16]{0,1:T(8,128)(2,1)} %param.13) | copy-start | bytes 294916
  10.9 81.2 %all-to-all-start.1 = ((bf16[32,3072,16]{1,2,0:T(8,128)(2,1)}), bf16[32,3072,16]{1,2,0:T(8,128)(2,1)}, u32[]{:S(2)}, u32[]{:S(2)}) async-start(bf16[32,3072,16]{1,2,0:T(8,128)(2,1)} %stack.5), calls=%async_computation.2 | async-start | bytes 6291456 | tf_op jit(solution)/shard_map/all_to_all | solution.py:61
  94.1 75.4 %all-to-all-start = ((bf16[32,3072,16]{1,2,0:T(8,128)(2,1)}), bf16[32,3072,16]{1,2,0:T(8,128)(2,1)}, u32[]{:S(2)}, u32[]{:S(2)}) async-start(bf16[32,3072,16]{1,2,0:T(8,128)(2,1)} %stack.4), calls=%async_computation | async-start | bytes 6291456 | tf_op jit(solution)/shard_map/all_to_all | solution.py:61
  103.1 157.0 %all-reduce.7.cloned.1.call-start = ((), (), s32[]{:S(2)}) async-start(), calls=%async_computation.7 | async-start | bytes 3145728 | tf_op jit(solution)/shard_map/psum | solution.py:11
  171.7 193.9 %reduce-scatter.3.cloned.1.call-start = ((), (), s32[]{:S(2)}) async-start(), calls=%async_computation.4 | async-start | bytes 3244032 | tf_op jit(solution)/shard_map/reduce_scatter | solution.py:66
  260.1 8.4 %copy-start.10 = (bf16[768,512]{0,1:T(8,128)(2,1)S(1)}, bf16[768,512]{0,1:T(8,128)(2,1)}, u32[]{:S(2)}) copy-start(bf16[768,512]{0,1:T(8,128)(2,1)} %get-tuple-element.19) | copy-start | bytes 2359300
  268.5 194.7 %reduce-scatter.5.cloned.1.call-start = ((), (), s32[]{:S(2)}) async-start(), calls=%async_computation.5 | async-start | bytes 3244032 | tf_op jit(solution)/shard_map/reduce_scatter | solution.py:66
  276.4 190.3 %copy-start.6 = (f32[512,512]{1,0:T(8,128)S(1)}, f32[512,512]{1,0:T(8,128)}, u32[]{:S(2)}) copy-start(f32[512,512]{1,0:T(8,128)} %param.17) | copy-start | bytes 3145732
  276.4 456.1 %all-reduce.5.cloned.1.call-start = ((), (), s32[]{:S(2)}) async-start(), calls=%async_computation.6 | async-start | bytes 6291456 | tf_op jit(solution)/shard_map/psum | solution.py:76
  366.5 101.6 %copy-start.4 = (bf16[96,512]{1,0:T(8,128)(2,1)}, bf16[96,512]{1,0:T(8,128)(2,1)S(1)}, u32[]{:S(2)}) copy-start(bf16[96,512]{1,0:T(8,128)(2,1)S(1)} %negate_convert_fusion) | copy-start | bytes 294916
  366.5 366.1 %copy-start.5 = (f32[512,512]{1,0:T(8,128)S(1)}, f32[512,512]{1,0:T(8,128)}, u32[]{:S(2)}) copy-start(f32[512,512]{1,0:T(8,128)} %param.16) | copy-start | bytes 3145732
  464.3 269.8 %copy-start.8 = (bf16[96,512]{1,0:T(8,128)(2,1)}, bf16[96,512]{1,0:T(8,128)(2,1)S(1)}, u32[]{:S(2)}) copy-start(bf16[96,512]{1,0:T(8,128)(2,1)S(1)} %fusion.6) | copy-start | bytes 294916
  732.6 4.2 copy-start.3
  732.6 4.2 copy-start.7
  734.2 7.2 copy-start.1
  736.8 4.6 copy-start.2
Sparse Core Ops, SparseCore 0:
  171.9 88.1 all-reduce.6
  268.6 96.9 reduce-scatter.2
  370.0 93.1 reduce-scatter.4
  469.4 263.1 all-reduce.4
